TPU v7x, 256 devices: a whole 4x4x8 slice. The times are simulated.
256 devices in a mesh: slab: 256 (over z, x, y, core).
Axes of the slice: x: 4, y: 4, z: 8, core: 2. Of those that a mesh axis runs over, the one named last changes fastest.
Arguments:
- newton_rhs: float32 [3, 1024, 128, 128], P(None, 'slab'), may hold values from -8 to 8
- stiffness: float32 [1024, 128, 128], P('slab'), may hold values from 0.25 to 4
- stencil: float32 [27, 3, 3], replicated, may hold values from -0.1 to 10.1, as said below
- dual_weight: float32 [1024, 128], P('slab'), may hold values from 0.5 to 2
- mortar: bfloat16 [1024, 3, 128, 128], P('slab'), may hold values from -0.3125 to 0.3125
- partner: int32 [1024, 3], P('slab'), may hold values from 0 to 1023, as said below
- active: int32 [1024], P('slab'), may hold values 0 or 1
Outputs:
- increment: float32 [3, 1024, 128, 128], P(None, 'slab')
- residual: float32 [3, 1024, 128, 128], P(None, 'slab')
Inputs may be any that keep to these rules, and one draw needn't show every extreme that they name: stencil[26 - k] is the transpose of stencil[k]; entries off the centre block lie within 0.1 in magnitude, and the centre block stencil[13] is 10 times the identity plus a symmetric matrix of entries within 0.1. `partner`: slave tile t lies on device d = t // 4; slot s of it names a tile on device (1 - d // 128) * 128 + (d % 128 + s - 1) modulo 128.
All inputs are finite; a program needn't handle non-finite values. No bound on the sum of `active` on one device may be relied on, other than what follows from the above.
Results may differ from a plain program's by a relative error of at most 0.0003.
Values sent between devices are 32-bit elements; how exact they have to be, the bound alone decides.
No kernel may reach another device: no remote copies, remote signals or barrier semaphores. Data moves between devices by JAX's collectives and lax.ppermute only.
A program may use at most 64 MiB of HBM per device.

v0:
```python
import jax
import jax.numpy as jnp
from jax import lax
from jax.sharding import PartitionSpec as P

ITERS = 2


def with_halo(array, sides, width):
    for axis, dim in sides:
        peers, length = (lax.axis_size(axis), array.shape[dim])
        up = [(i, (i + 1) % peers) for i in range(peers)]
        down = [(j, i) for i, j in up]
        last = lax.slice_in_dim(array, length - width, length, axis=dim)
        initial = lax.slice_in_dim(array, 0, width, axis=dim)
        before = lax.ppermute(last, axis, up)
        after = lax.ppermute(initial, axis, down)
        array = jnp.concatenate([before, array, after], axis=dim)
    return array


def stencil_part(field_in, stencil):
    padded = with_halo(field_in, (("slab", 1),), 1)
    slab_index = lax.axis_index("slab")
    quarter_count = lax.axis_size("slab") // 4
    lower_cut = jnp.logical_or(slab_index == quarter_count, slab_index == 3 * quarter_count)
    upper_cut = jnp.logical_or(slab_index == quarter_count - 1, slab_index == 3 * quarter_count - 1)
    lower_rim = jnp.where(lower_cut, 0.0, padded[:, :1])
    upper_rim = jnp.where(upper_cut, 0.0, padded[:, -1:])
    padded = jnp.concatenate([lower_rim, padded[:, 1:-1], upper_rim], axis=1)
    padded = jnp.pad(padded, ((0, 0), (0, 0), (1, 1), (1, 1)))
    plane_count = field_in.shape[1]
    node_count = field_in.shape[2]
    depth_count = field_in.shape[3]
    outputs = [jnp.zeros(field_in.shape[1:], jnp.float32) for out_comp in range(3)]
    for along_x in range(3):
        for along_y in range(3):
            for along_z in range(3):
                offset_index = 9 * along_x + 3 * along_y + along_z
                window_view = padded[
                    :,
                    along_x : along_x + plane_count,
                    along_y : along_y + node_count,
                    along_z : along_z + depth_count,
                ]
                for out_comp in range(3):
                    for in_comp in range(3):
                        outputs[out_comp] = (
                            outputs[out_comp]
                            + stencil[offset_index, out_comp, in_comp] * window_view[in_comp]
                        )
    return jnp.stack(outputs)


def contact_gather(master, slave_face, dual_weight, mortar_full, partner, active_float):
    planes = master.shape[0]
    tile_width = master.shape[1]
    all_faces = lax.all_gather(master, "slab", axis=0, tiled=True)
    facing = jnp.take(all_faces, partner, axis=0)
    pulled = jnp.einsum("tpij,tpj->ti", mortar_full, facing, precision=lax.Precision.HIGHEST)
    push_force = 4.0 * active_float[:, None] * (dual_weight * slave_face - pulled)
    back_force = -jnp.einsum(
        "tpij,ti->tpj", mortar_full, push_force, precision=lax.Precision.HIGHEST
    )
    reaction_table = jnp.zeros((planes * lax.axis_size("slab"), tile_width), jnp.float32)
    reaction_table = reaction_table.at[partner.reshape(-1)].add(back_force.reshape(-1, tile_width))
    master_add = lax.psum_scatter(reaction_table, "slab", scatter_dimension=0, tiled=True)
    return (dual_weight * push_force, master_add)


def apply_operator(field_in, stencil, stiffness, dual_weight, mortar_full, partner, active_float):
    result = stencil_part(field_in, stencil) + stiffness[None] * field_in
    slave_face = field_in[2, :, :, -1]
    master = field_in[2, :, :, 0]
    slave_add, master_add = contact_gather(
        master, slave_face, dual_weight, mortar_full, partner, active_float
    )
    result = result.at[2, :, :, -1].add(slave_add)
    result = result.at[2, :, :, 0].add(master_add)
    return result


def residual_squares(residual):
    return lax.psum(jnp.sum(residual * residual), "slab")


def local(newton_rhs, stiffness, stencil, dual_weight, mortar, partner, active):
    mortar_full = mortar.astype(jnp.float32)
    active_float = active.astype(jnp.float32)
    increment = jnp.zeros_like(newton_rhs)
    residual = newton_rhs
    direction = newton_rhs
    norm_now = residual_squares(residual)
    for iteration in range(ITERS):
        image = apply_operator(
            direction, stencil, stiffness, dual_weight, mortar_full, partner, active_float
        )
        curvature = lax.psum(jnp.sum(direction * image), "slab")
        step_size = norm_now / curvature
        increment = increment + step_size * direction
        residual = residual - step_size * image
        norm_next = residual_squares(residual)
        direction = residual + norm_next / norm_now * direction
        norm_now = norm_next
    return (increment, residual)


def solution(mesh):
    placed = (
        P(None, "slab", None, None),
        P("slab", None, None),
        P(),
        P("slab", None),
        P("slab", None, None, None),
        P("slab", None),
        P("slab"),
    )
    return jax.shard_map(
        local,
        mesh=mesh,
        in_specs=placed,
        out_specs=(P(None, "slab", None, None), P(None, "slab", None, None)),
        check_vma=False,
    )
```

profile of v0, /device:TPU:1, one launch (start us, length us, event | category | flops | bytes accessed | tf_op | source)
XLA Modules:
  0.0 1311.5 jit_solution(6436635839375762363)
XLA Ops:
  8.5 3.3 collective-permute-start.1
  15.4 1.9 fusion.38
  17.3 2.1 fusion.26
  19.4 2.1 fusion.34
  21.5 1.8 fusion.33
  23.3 2.1 fusion.32
  25.4 2.1 fusion.31
  27.5 2.1 fusion.30
  29.6 2.1 fusion.29
  31.6 1.8 fusion.28
  33.5 2.1 fusion.27
  35.6 2.1 fusion.37
  37.7 2.1 fusion.36
  39.8 2.1 fusion.35
  44.7 75.9 %all-gather = f32[1,1024,128,1]{2,3,0,1:T(1,128)S(1)} all-gather(f32[1,4,128,1]{2,3,0,1:T(1,128)S(1)} %copy.72), channel_id=2, replica_groups=mesh['slab'=256] {'slab'}, dimensions={1}, use_global_device_ids=true | all-gather | bytes 526336 | tf_op jit(solution)/shard_map/all_gather | solution.py:58
  122.2 2.5 select_maximum_fusion.2
  124.7 59.7 %multiply_add_fusion.7 = (f32[1,4,128,128]{2,1,3,0:T(4,128)S(1)}, f32[1,4,128,128]{2,1,3,0:T(4,128)S(1)}, f32[1,4,128,128]{2,1,3,0:T(4,128)S(1)}, f32[1,4,128,12...) fusion(f32[3,6,130,130]{2,1,3,0:T(8,128)S(1)} %select_maximum_f, ...), kind=kLoop, calls=%fused_computation.50 | loop fusion | flops 10944512 | bytes 22675780 | tf_op jit(solution)/shard_map/add | solution.py:49
  184.4 59.1 %multiply_add_fusion.6 = f32[1,4,128,128]{2,1,3,0:T(4,128)S(1)} fusion(f32[1,4,128,128]{2,1,3,0:T(4,128)S(1)} %get-tuple-element.76, f32[1,4,128,128]{2,1,3,0:T(4,128)S(1)} %get-tuple-element.75, f32[1,4,128,128]{2,1,3,0:T(4,128)S(1)} %get-tuple-element.74, f32[1,4,128,128]{2,1,3,0:T(4,128)S(1)} %get-tuple-element.73, ...), kind=kLoop, calls=%fused_computation.49 | loop fusion | flops 10551296 | bytes 21496132 | tf_op jit(solution)/shard_map/add | solution.py:49
  243.5 59.0 %multiply_add_fusion.5 = f32[1,4,128,128]{2,1,3,0:T(4,128)S(1)} fusion(f32[1,4,128,128]{2,1,3,0:T(4,128)S(1)} %get-tuple-element.76, f32[1,4,128,128]{2,1,3,0:T(4,128)S(1)} %get-tuple-element.75, f32[1,4,128,128]{2,1,3,0:T(4,128)S(1)} %get-tuple-element.74, f32[1,4,128,128]{2,1,3,0:T(4,128)S(1)} %get-tuple-element.73, ...), kind=kLoop, calls=%fused_computation.48 | loop fusion | flops 10551296 | bytes 21496132 | tf_op jit(solution)/shard_map/add | solution.py:49
  305.6 246.9 %all-reduce.8.cloned.1.call-done = f32[1024,128]{1,0:T(8,128)} async-done(((f32[1024,128]{1,0:T(8,128)}), f32[1024,128]{1,0:T(8,128)}) %all-reduce.8.cloned.1.call-update) | async-done | bytes 524304
  554.2 77.8 %all-reduce.4 = (f32[]{:T(128)}, f32[]{:T(128)}) all-reduce(f32[]{:T(128)} %multiply_reduce_fusion.3, f32[]{:T(128)} %multiply_reduce_fusion.2), channel_id=1, replica_groups=mesh['slab'=256] {'slab'}, use_global_device_ids=true, to_apply=%region_1.0 | all-reduce | flops 2 | bytes 16 | tf_op jit(solution)/shard_map/psum | solution.py:84
  634.4 73.2 %psum.30 = f32[]{:T(128)} all-reduce(f32[]{:T(128)} %multiply_reduce_fusion.1), channel_id=1, replica_groups=mesh['slab'=256] {'slab'}, use_global_device_ids=true, to_apply=%region_7.9 | all-reduce | flops 1 | bytes 8 | tf_op jit(solution)/shard_map/psum | solution.py:84
  711.4 72.0 %all-gather.1 = f32[1,1024,128,1]{2,3,0,1:T(1,128)S(1)} all-gather(f32[1,4,128,1]{2,3,0,1:T(1,128)S(1)} %bitcast.335), channel_id=3, replica_groups=mesh['slab'=256] {'slab'}, dimensions={1}, use_global_device_ids=true | all-gather | bytes 526336 | tf_op jit(solution)/shard_map/all_gather | solution.py:58
  785.9 2.5 select_maximum_fusion
  788.4 59.4 %multiply_add_fusion.4 = (f32[1,4,128,128]{2,1,3,0:T(4,128)S(1)}, f32[1,4,128,128]{2,1,3,0:T(4,128)S(1)}, f32[1,4,128,128]{2,1,3,0:T(4,128)S(1)}, f32[1,4,128,12...) fusion(f32[3,6,130,130]{2,1,3,0:T(8,128)S(1)} %select_maximum_f, ...), kind=kLoop, calls=%fused_computation.43 | loop fusion | flops 10944512 | bytes 22675780 | tf_op jit(solution)/shard_map/add | solution.py:49
  847.9 59.1 %multiply_add_fusion.3 = f32[1,4,128,128]{2,1,3,0:T(4,128)S(1)} fusion(f32[1,4,128,128]{2,1,3,0:T(4,128)S(1)} %get-tuple-element.67, f32[1,4,128,128]{2,1,3,0:T(4,128)S(1)} %get-tuple-element.66, f32[1,4,128,128]{2,1,3,0:T(4,128)S(1)} %get-tuple-element.65, f32[1,4,128,128]{2,1,3,0:T(4,128)S(1)} %get-tuple-element.64, ...), kind=kLoop, calls=%fused_computation.42 | loop fusion | flops 10551296 | bytes 21496132 | tf_op jit(solution)/shard_map/add | solution.py:49
  907.0 59.0 %multiply_add_fusion.2 = f32[1,4,128,128]{2,1,3,0:T(4,128)S(1)} fusion(f32[1,4,128,128]{2,1,3,0:T(4,128)S(1)} %get-tuple-element.67, f32[1,4,128,128]{2,1,3,0:T(4,128)S(1)} %get-tuple-element.66, f32[1,4,128,128]{2,1,3,0:T(4,128)S(1)} %get-tuple-element.65, f32[1,4,128,128]{2,1,3,0:T(4,128)S(1)} %get-tuple-element.64, ...), kind=kLoop, calls=%fused_computation.41 | loop fusion | flops 10551296 | bytes 21496132 | tf_op jit(solution)/shard_map/add | solution.py:49
  966.8 1.5 scatter_custom_fusion.1
  968.3 249.6 %all-reduce.10.cloned.1.call-done = f32[1024,128]{1,0:T(8,128)} async-done(((f32[1024,128]{1,0:T(8,128)}), f32[1024,128]{1,0:T(8,128)}) %all-reduce.10.cloned.1.call-update) | async-done | bytes 524304
  1219.6 77.6 %psum.31 = f32[]{:T(128)} all-reduce(f32[]{:T(128)} %multiply_reduce_fusion), channel_id=1, replica_groups=mesh['slab'=256] {'slab'}, use_global_device_ids=true, to_apply=%region_11.13 | all-reduce | flops 1 | bytes 8 | tf_op jit(solution)/shard_map/psum | solution.py:98
  1299.9 2.3 copy.62
  1302.2 2.3 copy.63
  (75 shorter events, 23.7 us)
Async XLA Ops:
  7.2 114.1 %copy-start = (bf16[4,3,128,128]{3,2,1,0:T(8,128)(2,1)S(1)}, bf16[4,3,128,128]{3,2,1,0:T(8,128)(2,1)}, u32[]{:S(2)}) copy-start(bf16[4,3,128,128]{3,2,1,0:T(8,128)(2,1)} %param.21) | copy-start | bytes 1179652
  7.2 37.1 %copy-start.6 = (s32[4]{0:T(128)S(1)}, s32[4]{0:T(128)}, u32[]{:S(2)}) copy-start(s32[4]{0:T(128)} %param.23) | copy-start | bytes 52
  7.2 37.2 %copy-start.4 = (f32[4,128,128]{2,1,0:T(8,128)S(1)}, f32[4,128,128]{2,1,0:T(8,128)}, u32[]{:S(2)}) copy-start(f32[4,128,128]{2,1,0:T(8,128)} %param.18) | copy-start | bytes 786436
  7.2 545.3 %all-reduce.8.cloned.1.call-start = ((), (), s32[]{:S(2)}) async-start(), calls=%async_computation | async-start | bytes 1048576
  8.5 113.3 %collective-permute-start.1 = (f32[3,1,128,128]{2,1,3,0:T(1,128)S(1)}, f32[3,1,128,128]{2,1,3,0:T(1,128)S(1)}, u32[]{:S(2)}, u32[]{:S(2)}) collective-permute-start(f32[3,1,128,128]{2,1,3,0:T(1,128)S(1)} %copy.46), channel_id=1, source_target_pairs={{1,0},{2,1},{3,2},{4,3},{5,4},{6,5},{7,6},{8,7},{9,8},{10,9},{11,1... | collective-permute-start | bytes 589832 | tf_op jit(solution)/shard_map/ppermute | solution.py:17
  11.9 110.1 %collective-permute-start = (f32[3,1,128,128]{2,1,3,0:T(1,128)S(1)}, f32[3,1,128,128]{2,1,3,0:T(1,128)S(1)}, u32[]{:S(2)}, u32[]{:S(2)}) collective-permute-start(f32[3,1,128,128]{2,1,3,0:T(1,128)S(1)} %copy.45), channel_id=1, source_target_pairs={{0,1},{1,2},{2,3},{3,4},{4,5},{5,6},{6,7},{7,8},{8,9},{9,10},{10,1... | collective-permute-start | bytes 589832 | tf_op jit(solution)/shard_map/ppermute | solution.py:16
  44.5 258.0 %copy-start.2 = (f32[4,128,128]{1,0,2:T(4,128)}, f32[4,128,128]{1,0,2:T(4,128)S(1)}, u32[]{:S(2)}) copy-start(f32[4,128,128]{1,0,2:T(4,128)S(1)} %copy.53) | copy-start | bytes 786436
  121.8 181.5 %copy-start.7 = (s32[12]{0:T(128)}, s32[12]{0:T(128)S(1)}, u32[]{:S(2)}) copy-start(s32[12]{0:T(128)S(1)} %fusion.21) | copy-start | bytes 148
  243.5 59.3 %copy-start.5 = (f32[4,128]{1,0:T(4,128)S(1)}, f32[4,128]{1,0:T(4,128)}, u32[]{:S(2)}) copy-start(f32[4,128]{1,0:T(4,128)} %param.20) | copy-start | bytes 6148
  302.5 2.3 copy-start.1
  304.7 913.2 %all-reduce.10.cloned.1.call-start = ((), (), s32[]{:S(2)}) async-start(), calls=%async_computation.1 | async-start | bytes 1048576
  710.2 74.4 %collective-permute-start.2 = (f32[3,1,128,128]{2,1,3,0:T(1,128)}, f32[3,1,128,128]{2,1,3,0:T(1,128)}, u32[]{:S(2)}, u32[]{:S(2)}) collective-permute-start(f32[3,1,128,128]{2,1,3,0:T(1,128)} %get-tuple-element.79), channel_id=1, source_target_pairs={{0,1},{1,2},{2,3},{3,4},{4,5},{5,6},{6,7},{7,8},{8,9},{9,10},{10,1... | collective-permute-start | bytes 589832 | tf_op jit(solution)/shard_map/ppermute | solution.py:16
  711.4 74.3 %collective-permute-start.3 = (f32[3,1,128,128]{2,1,3,0:T(1,128)}, f32[3,1,128,128]{2,1,3,0:T(1,128)S(1)}, u32[]{:S(2)}, u32[]{:S(2)}) collective-permute-start(f32[3,1,128,128]{2,1,3,0:T(1,128)} %get-tuple-element.80), channel_id=1, source_target_pairs={{1,0},{2,1},{3,2},{4,3},{5,4},{6,5},{7,6},{8,7},{9,8},{10,9},{11,1... | collective-permute-start | bytes 589832 | tf_op jit(solution)/shard_map/ppermute | solution.py:17
  907.0 59.0 %copy-start.3 = (f32[4,128,128]{1,0,2:T(4,128)S(1)}, f32[4,128,128]{1,0,2:T(4,128)}, u32[]{:S(2)}) copy-start(f32[4,128,128]{1,0,2:T(4,128)} %copy-done.2) | copy-start | bytes 786436
Sparse Core Ops, SparseCore 0:
  304.8 247.6 all-reduce.7
  968.4 249.4 all-reduce.9
where the time goes:
time: 1320 us; the launch traced here: 1310 us
  waiting for transfers between devices  497 us (38%)
  blocking collectives  377 us (29%)
  other arithmetic  374 us (28%)
  local copies, waits for them, and re-layouts  39.3 us (3%)
  between operations  18.7 us (1%)
    unnamed x4, waiting for transfers between devices  496 us
    add x6, other arithmetic, stencil_part(): outputs[out_comp]  355 us
    psum x2, blocking collectives, residual_squares(): return lax.psum(jnp.sum(residual * residual), 'slab')  151 us
    all_gather x2, blocking collectives, contact_gather(): all_faces = lax.all_gather(master, 'slab', axis=0, tiled=True)  148 us
    psum x1, blocking collectives, local(): curvature = lax.psum(jnp.sum(direction * image), 'slab')  77.6 us
    slice x14, local copies, waits for them, and re-layouts, stencil_part(): stencil[offset_index, out_comp, in_comp] * window_view[in_comp]  27.6 us
  transfers between devices with their start and end apart: 6, of which 2 were waited for; matrix products, arithmetic and copies ran while one was open for 3% of the time, Pallas kernels for 0%

commit v1 on v0

--- a/solution.py
+++ b/solution.py
@@ -55,7 +55,9 @@
 def contact_gather(master, slave_face, dual_weight, mortar_full, partner, active_float):
     planes = master.shape[0]
     tile_width = master.shape[1]
-    all_faces = lax.all_gather(master, "slab", axis=0, tiled=True)
+    all_faces = jnp.concatenate(
+        lax.all_to_all(jnp.stack([master] * lax.axis_size("slab")), "slab", 0, 0), axis=0
+    )
     facing = jnp.take(all_faces, partner, axis=0)
     pulled = jnp.einsum("tpij,tpj->ti", mortar_full, facing, precision=lax.Precision.HIGHEST)
     push_force = 4.0 * active_float[:, None] * (dual_weight * slave_face - pulled)

time: 1320 us -> 1200 us (0.909)
  blocking collectives: 377 us -> 229 us
  starting transfers between devices: 4.7 us -> 35.3 us
  local copies, waits for them, and re-layouts: 39.3 us -> 22.7 us
  waiting for transfers between devices: 497 us -> 511 us
    all_gather x2 -> x0, blocking collectives: 148 us -> none  [contact_gather(): all_faces = lax.all_gather(master, 'slab', axis=0, tiled=True)]
    all_to_all x0 -> x2, starting transfers between devices: none -> 30.6 us  [contact_gather(): lax.all_to_all(jnp.stack([master] * lax.axis_size('slab')), 'slab', 0, 0)]
    slice x14, local copies, waits for them, and re-layouts: 27.6 us -> 10 us  [stencil_part(): stencil[offset_index, out_comp, in_comp] * window_view[in_comp]]
    unnamed x4, waiting for transfers between devices: 496 us -> 511 us
  transfers between devices with their start and end apart: 6 -> 8, of which waited for: 2 -> 2; matrix products, arithmetic and copies ran while one was open for 3% -> 32% of each run, Pallas kernels for 0% -> 0%
where the time goes in v1:
time: 1200 us; the launch traced here: 1190 us
  waiting for transfers between devices  511 us (43%)
  other arithmetic  375 us (31%)
  blocking collectives  229 us (19%)
  starting transfers between devices  35.3 us (3%)
  local copies, waits for them, and re-layouts  22.7 us (2%)
  between operations  18.6 us (2%)
    unnamed x4, waiting for transfers between devices  511 us
    add x6, other arithmetic, stencil_part(): outputs[out_comp]  356 us
    psum x2, blocking collectives, residual_squares(): return lax.psum(jnp.sum(residual * residual), 'slab')  151 us
    psum x1, blocking collectives, local(): curvature = lax.psum(jnp.sum(direction * image), 'slab')  77.6 us
    all_to_all x2, starting transfers between devices, contact_gather(): lax.all_to_all(jnp.stack([master] * lax.axis_size('slab')), 'slab', 0, 0)  30.6 us
  transfers between devices with their start and end apart: 8, of which 2 were waited for; matrix products, arithmetic and copies ran while one was open for 32% of the time, Pallas kernels for 0%

profile of v1, /device:TPU:1, one launch (start us, length us, event | category | flops | bytes accessed | tf_op | source)
XLA Modules:
  0.0 1193.3 jit_solution(12898774450962638769)
XLA Ops:
  7.2 1.2 fusion.25
  8.5 3.3 collective-permute-start.1
  12.6 1.1 slice_reduce_fusion
  13.7 0.9 stack.9
  14.6 17.4 %all-to-all-start = ((f32[256,4,128]{2,1,0:T(4,128)}), f32[256,4,128]{2,1,0:T(4,128)S(1)}, u32[]{:S(2)}, u32[]{:S(2)}) async-start(f32[256,4,128]{2,1,0:T(4,128)} %stack.9), calls=%async_computation | async-start | bytes 1048576 | tf_op jit(solution)/shard_map/all_to_all | solution.py:59
  43.7 1.1 broadcast_select_fusion.3
  44.8 2.5 select_maximum_fusion.2
  47.3 59.9 %multiply_add_fusion.7 = (f32[1,4,128,128]{2,1,3,0:T(4,128)S(1)}, f32[1,4,128,128]{2,1,3,0:T(4,128)S(1)}, f32[1,4,128,128]{2,1,3,0:T(4,128)S(1)}, f32[1,4,128,12...) fusion(f32[3,6,130,130]{2,1,3,0:T(8,128)S(1)} %select_maximum_f, ...), kind=kLoop, calls=%fused_computation.51 | loop fusion | flops 10944512 | bytes 22675780 | tf_op jit(solution)/shard_map/add | solution.py:49
  107.2 59.0 %multiply_add_fusion.6 = f32[1,4,128,128]{2,1,3,0:T(4,128)S(1)} fusion(f32[1,4,128,128]{2,1,3,0:T(4,128)S(1)} %get-tuple-element.74, f32[1,4,128,128]{2,1,3,0:T(4,128)S(1)} %get-tuple-element.73, f32[1,4,128,128]{2,1,3,0:T(4,128)S(1)} %get-tuple-element.72, f32[1,4,128,128]{2,1,3,0:T(4,128)S(1)} %get-tuple-element.71, ...), kind=kLoop, calls=%fused_computation.50 | loop fusion | flops 10551296 | bytes 21496132 | tf_op jit(solution)/shard_map/add | solution.py:49
  166.2 59.1 %multiply_add_fusion.5 = f32[1,4,128,128]{2,1,3,0:T(4,128)S(1)} fusion(f32[1,4,128,128]{2,1,3,0:T(4,128)S(1)} %get-tuple-element.74, f32[1,4,128,128]{2,1,3,0:T(4,128)S(1)} %get-tuple-element.73, f32[1,4,128,128]{2,1,3,0:T(4,128)S(1)} %get-tuple-element.72, f32[1,4,128,128]{2,1,3,0:T(4,128)S(1)} %get-tuple-element.71, ...), kind=kLoop, calls=%fused_computation.49 | loop fusion | flops 10551296 | bytes 21496132 | tf_op jit(solution)/shard_map/add | solution.py:49
  227.3 1.5 scatter_custom_fusion
  228.8 0.9 multiply_reduce_fusion.3
  229.7 255.1 %all-reduce.8.cloned.1.call-done = f32[1024,128]{1,0:T(8,128)} async-done(((f32[1024,128]{1,0:T(8,128)}), f32[1024,128]{1,0:T(8,128)}) %all-reduce.8.cloned.1.call-update) | async-done | bytes 524304
  485.5 1.0 multiply_reduce_fusion.2
  486.5 77.8 %all-reduce.4 = (f32[]{:T(128)}, f32[]{:T(128)}) all-reduce(f32[]{:T(128)} %multiply_reduce_fusion.3, f32[]{:T(128)} %multiply_reduce_fusion.2), channel_id=1, replica_groups=mesh['slab'=256] {'slab'}, use_global_device_ids=true, to_apply=%region_1.0 | all-reduce | flops 2 | bytes 16 | tf_op jit(solution)/shard_map/psum | solution.py:86
  565.7 1.0 multiply_reduce_fusion.1
  566.7 73.3 %psum.30 = f32[]{:T(128)} all-reduce(f32[]{:T(128)} %multiply_reduce_fusion.1), channel_id=1, replica_groups=mesh['slab'=256] {'slab'}, use_global_device_ids=true, to_apply=%region_7.9 | all-reduce | flops 1 | bytes 8 | tf_op jit(solution)/shard_map/psum | solution.py:86
  641.7 1.3 collective-permute-start.2
  643.0 0.9 stack.21
  643.9 13.2 %all-to-all-start.1 = ((f32[256,4,128]{2,1,0:T(4,128)}), f32[256,4,128]{2,1,0:T(4,128)}, u32[]{:S(2)}, u32[]{:S(2)}) async-start(f32[256,4,128]{2,1,0:T(4,128)} %stack.21), calls=%async_computation.1 | async-start | bytes 1048576 | tf_op jit(solution)/shard_map/all_to_all | solution.py:59
  657.5 2.5 select_maximum_fusion
  660.0 59.7 %multiply_add_fusion.4 = (f32[1,4,128,128]{2,1,3,0:T(4,128)S(1)}, f32[1,4,128,128]{2,1,3,0:T(4,128)S(1)}, f32[1,4,128,128]{2,1,3,0:T(4,128)S(1)}, f32[1,4,128,12...) fusion(f32[3,6,130,130]{2,1,3,0:T(8,128)S(1)} %select_maximum_f, ...), kind=kLoop, calls=%fused_computation.43 | loop fusion | flops 10944512 | bytes 22675780 | tf_op jit(solution)/shard_map/add | solution.py:49
  719.7 59.0 %multiply_add_fusion.3 = f32[1,4,128,128]{2,1,3,0:T(4,128)S(1)} fusion(f32[1,4,128,128]{2,1,3,0:T(4,128)S(1)} %get-tuple-element.65, f32[1,4,128,128]{2,1,3,0:T(4,128)S(1)} %get-tuple-element.64, f32[1,4,128,128]{2,1,3,0:T(4,128)S(1)} %get-tuple-element.63, f32[1,4,128,128]{2,1,3,0:T(4,128)S(1)} %get-tuple-element.62, ...), kind=kLoop, calls=%fused_computation.42 | loop fusion | flops 10551296 | bytes 21496132 | tf_op jit(solution)/shard_map/add | solution.py:49
  778.7 59.1 %multiply_add_fusion.2 = f32[1,4,128,128]{2,1,3,0:T(4,128)S(1)} fusion(f32[1,4,128,128]{2,1,3,0:T(4,128)S(1)} %get-tuple-element.65, f32[1,4,128,128]{2,1,3,0:T(4,128)S(1)} %get-tuple-element.64, f32[1,4,128,128]{2,1,3,0:T(4,128)S(1)} %get-tuple-element.63, f32[1,4,128,128]{2,1,3,0:T(4,128)S(1)} %get-tuple-element.62, ...), kind=kLoop, calls=%fused_computation.41 | loop fusion | flops 10551296 | bytes 21496132 | tf_op jit(solution)/shard_map/add | solution.py:49
  838.2 1.6 gather_fusion.1
  842.1 1.5 scatter_custom_fusion.1
  843.7 256.1 %all-reduce.10.cloned.1.call-done = f32[1024,128]{1,0:T(8,128)} async-done(((f32[1024,128]{1,0:T(8,128)}), f32[1024,128]{1,0:T(8,128)}) %all-reduce.10.cloned.1.call-update) | async-done | bytes 524304
  1100.5 1.0 multiply_reduce_fusion
  1101.5 77.6 %psum.31 = f32[]{:T(128)} all-reduce(f32[]{:T(128)} %multiply_reduce_fusion), channel_id=1, replica_groups=mesh['slab'=256] {'slab'}, use_global_device_ids=true, to_apply=%region_11.13 | all-reduce | flops 1 | bytes 8 | tf_op jit(solution)/shard_map/psum | solution.py:100
  1180.3 1.3 multiply_subtract_fusion
  1181.6 2.3 copy.66
  1183.9 2.3 copy.67
  (84 shorter events, 19.3 us)
Async XLA Ops:
  7.2 219.1 %copy-start = (bf16[4,3,128,128]{3,2,1,0:T(8,128)(2,1)S(1)}, bf16[4,3,128,128]{3,2,1,0:T(8,128)(2,1)}, u32[]{:S(2)}) copy-start(bf16[4,3,128,128]{3,2,1,0:T(8,128)(2,1)} %param.21) | copy-start | bytes 1179652
  7.2 35.1 %copy-start.1 = (f32[3,4,128,128]{3,2,1,0:T(8,128)S(1)}, f32[3,4,128,128]{3,2,1,0:T(8,128)}, u32[]{:S(2)}) copy-start(f32[3,4,128,128]{3,2,1,0:T(8,128)} %param.17) | copy-start | bytes 2359300
  7.2 24.8 %copy-start.6 = (s32[4,3]{1,0:T(4,128)S(1)}, s32[4,3]{1,0:T(4,128)}, u32[]{:S(2)}) copy-start(s32[4,3]{1,0:T(4,128)} %param.22) | copy-start | bytes 148
  7.2 25.0 %copy-start.2 = (f32[27,3,3]{0,2,1:T(4,128)S(1)}, f32[27,3,3]{0,2,1:T(4,128)}, u32[]{:S(2)}) copy-start(f32[27,3,3]{0,2,1:T(4,128)} %param.19) | copy-start | bytes 2920
  7.2 35.4 %copy-start.10 = (s32[4]{0:T(128)S(1)}, s32[4]{0:T(128)}, u32[]{:S(2)}) copy-start(s32[4]{0:T(128)} %param.23) | copy-start | bytes 52
  7.2 35.5 %copy-start.5 = (f32[4,128,128]{2,1,0:T(8,128)S(1)}, f32[4,128,128]{2,1,0:T(8,128)}, u32[]{:S(2)}) copy-start(f32[4,128,128]{2,1,0:T(8,128)} %param.18) | copy-start | bytes 786436
  8.5 35.0 %collective-permute-start.1 = (f32[3,1,128,128]{2,1,3,0:T(1,128)S(1)}, f32[3,1,128,128]{2,1,3,0:T(1,128)S(1)}, u32[]{:S(2)}, u32[]{:S(2)}) collective-permute-start(f32[3,1,128,128]{2,1,3,0:T(1,128)S(1)} %copy.52), channel_id=1, source_target_pairs={{1,0},{2,1},{3,2},{4,3},{5,4},{6,5},{7,6},{8,7},{9,8},{10,9},{11,1... | collective-permute-start | bytes 589832 | tf_op jit(solution)/shard_map/ppermute | solution.py:17
  12.6 31.1 %collective-permute-start = (f32[3,1,128,128]{2,1,3,0:T(1,128)}, f32[3,1,128,128]{2,1,3,0:T(1,128)}, u32[]{:S(2)}, u32[]{:S(2)}) collective-permute-start(f32[3,1,128,128]{2,1,3,0:T(1,128)} %copy.51), channel_id=1, source_target_pairs={{0,1},{1,2},{2,3},{3,4},{4,5},{5,6},{6,7},{7,8},{8,9},{9,10},{10,1... | collective-permute-start | bytes 589832 | tf_op jit(solution)/shard_map/ppermute | solution.py:16
  14.6 211.1 %all-to-all-start = ((f32[256,4,128]{2,1,0:T(4,128)}), f32[256,4,128]{2,1,0:T(4,128)S(1)}, u32[]{:S(2)}, u32[]{:S(2)}) async-start(f32[256,4,128]{2,1,0:T(4,128)} %stack.9), calls=%async_computation | async-start | bytes 1048576 | tf_op jit(solution)/shard_map/all_to_all | solution.py:59
  32.0 452.8 %all-reduce.8.cloned.1.call-start = ((), (), s32[]{:S(2)}) async-start(), calls=%async_computation.2 | async-start | bytes 1048576
  32.1 194.2 %copy-start.8 = (pred[4,3]{1,0:T(4,128)(4,1)}, pred[4,3]{1,0:T(4,128)(4,1)S(1)}, u32[]{:S(2)}) copy-start(pred[4,3]{1,0:T(4,128)(4,1)S(1)} %compare_and_fusion) | copy-start | bytes 40
  42.6 184.2 %copy-start.9 = (f32[4]{0:T(128)}, f32[4]{0:T(128)S(1)}, u32[]{:S(2)}) copy-start(f32[4]{0:T(128)S(1)} %convert_multiply_fusion) | copy-start | bytes 52
  42.9 182.5 %copy-start.3 = (f32[4,128,128]{1,0,2:T(4,128)}, f32[4,128,128]{1,0,2:T(4,128)S(1)}, u32[]{:S(2)}) copy-start(f32[4,128,128]{1,0,2:T(4,128)S(1)} %copy.59) | copy-start | bytes 786436
  166.2 60.6 %copy-start.7 = (f32[4,128]{1,0:T(4,128)S(1)}, f32[4,128]{1,0:T(4,128)}, u32[]{:S(2)}) copy-start(f32[4,128]{1,0:T(4,128)} %param.20) | copy-start | bytes 6148
  641.7 15.4 %collective-permute-start.2 = (f32[3,1,128,128]{2,1,3,0:T(1,128)S(1)}, f32[3,1,128,128]{2,1,3,0:T(1,128)S(1)}, u32[]{:S(2)}, u32[]{:S(2)}) collective-permute-start(f32[3,1,128,128]{2,1,3,0:T(1,128)S(1)} %get-tuple-element.77), channel_id=1, source_target_pairs={{0,1},{1,2},{2,3},{3,4},{4,5},{5,6},{6,7},{7,8},{8,9},{9,10},{10,1... | collective-permute-start | bytes 589832 | tf_op jit(solution)/shard_map/ppermute | solution.py:16
  643.0 14.3 %collective-permute-start.3 = (f32[3,1,128,128]{2,1,3,0:T(1,128)S(1)}, f32[3,1,128,128]{2,1,3,0:T(1,128)S(1)}, u32[]{:S(2)}, u32[]{:S(2)}) collective-permute-start(f32[3,1,128,128]{2,1,3,0:T(1,128)S(1)} %get-tuple-element.78), channel_id=1, source_target_pairs={{1,0},{2,1},{3,2},{4,3},{5,4},{6,5},{7,6},{8,7},{9,8},{10,9},{11,1... | collective-permute-start | bytes 589832 | tf_op jit(solution)/shard_map/ppermute | solution.py:17
  643.9 194.3 %all-to-all-start.1 = ((f32[256,4,128]{2,1,0:T(4,128)}), f32[256,4,128]{2,1,0:T(4,128)}, u32[]{:S(2)}, u32[]{:S(2)}) async-start(f32[256,4,128]{2,1,0:T(4,128)} %stack.21), calls=%async_computation.1 | async-start | bytes 1048576 | tf_op jit(solution)/shard_map/all_to_all | solution.py:59
  657.1 442.7 %all-reduce.10.cloned.1.call-start = ((), (), s32[]{:S(2)}) async-start(), calls=%async_computation.3 | async-start | bytes 1048576
  778.7 59.1 %copy-start.4 = (f32[4,128,128]{1,0,2:T(4,128)S(1)}, f32[4,128,128]{1,0,2:T(4,128)}, u32[]{:S(2)}) copy-start(f32[4,128,128]{1,0,2:T(4,128)} %copy-done.3) | copy-start | bytes 786436
Sparse Core Ops, SparseCore 0:
  228.9 255.8 all-reduce.7
  843.8 255.9 all-reduce.9
